TPU v7x, 32 devices: a whole 2x2x4 slice. The times are simulated.
32 devices in a mesh: pts: 8 (over z, y), feat: 4 (over x, core).
Axes of the slice: x: 2, y: 2, z: 4, core: 2. Of those that a mesh axis runs over, the one named last changes fastest.
Arguments:
- slab: bfloat16 [16384, 768], P('pts', 'feat'), may hold values from -40 to 40
- centres: bfloat16 [4096, 768], replicated, may hold values from -3 to 3
- labels: int32 [16384, 1], P(('pts', 'feat')), may hold values from 0 to 4095
- sample_rows: int32 [8, 8, 4], P('pts'), may hold values from 0 to 2047, as said below
- sample_count: int32 [8, 8], P('pts'), may hold values from 0 to 4, as said below
- slot_offset: int32 [8, 8], P('pts'), may hold values from 0 to 28, as said below
Outputs:
- coreset: bfloat16 [256, 768], P('pts', 'feat')
Inputs may be any that keep to these rules, and one draw needn't show every extreme that they name: `sample_rows`: row indices within a source shard; sampled independently with replacement. `sample_count`: in every draw some owner receives 4 rows from every source. slot_offset[o,p] is the sum of sample_count[q,o] over sources q < p.
All inputs are finite; a program needn't handle non-finite values.
Results may differ from a plain program's by a relative error of at most 0.0006.
Values may be sent and summed in bfloat16 or wider, within the bound.
A program may use at most 64 MiB of HBM per device.

v0:
```python
import jax
import jax.numpy as jnp
from jax import lax
from jax.sharding import PartitionSpec as P


def local(slab, centres, labels, sample_rows, sample_count, slot_offset):
    rows_pts, feat_width = slab.shape
    feat_count = lax.axis_size("feat")
    rows_dev = rows_pts // feat_count
    centre_count = centres.shape[0]
    contract = (((1,), (1,)), ((), ()))
    centre_sq = jnp.sum(jnp.square(centres.astype(jnp.float32)), axis=1)
    stacked = slab.reshape(feat_count, rows_dev, feat_width)
    points = lax.all_to_all(stacked, "feat", split_axis=0, concat_axis=2, tiled=True)[0]
    cross_term = lax.dot_general(points, centres, contract, preferred_element_type=jnp.float32)
    point_sq = jnp.sum(jnp.square(points.astype(jnp.float32)), axis=1)
    nearest = jnp.min(point_sq[:, None] + centre_sq[None, :] - 2.0 * cross_term, axis=1)[None, :][0]
    member = labels[:, 0]
    cost_part = jax.ops.segment_sum(nearest, member, num_segments=centre_count)
    size_part = jax.ops.segment_sum(jnp.ones_like(nearest), member, num_segments=centre_count)
    cluster_cost, cluster_size = lax.psum((cost_part, size_part), ("pts", "feat"))
    own_sens = nearest / jnp.take(cluster_cost, member) + 1.0 / jnp.take(cluster_size, member)
    shard_sens = lax.all_gather(own_sens, "feat", axis=0, tiled=True)
    total_points = rows_pts * lax.axis_size("pts")
    weight = 2.0 * centre_count / total_points / shard_sens
    picked_rows = sample_rows[0]
    owner_count, slot_count = picked_rows.shape
    chosen = jnp.take(slab, picked_rows.reshape(-1), axis=0).reshape(
        owner_count, slot_count, feat_width
    )
    chosen_weight = jnp.take(weight, picked_rows)
    live_slot = jnp.arange(slot_count, dtype=jnp.int32)[None, :] < sample_count[0][:, None]
    scaled = jnp.where(
        live_slot[:, :, None], chosen.astype(jnp.float32) * chosen_weight[:, :, None], 0.0
    ).astype(jnp.bfloat16)
    arrived = lax.all_to_all(scaled, "pts", split_axis=0, concat_axis=0, tiled=True)
    target = slot_offset[0][:, None] + jnp.arange(slot_count, dtype=jnp.int32)[None, :]
    own_rows = arrived.shape[0] * slot_count
    placed = jnp.zeros((own_rows, feat_width), jnp.float32)
    placed = placed.at[target.reshape(-1)].add(
        arrived.reshape(-1, feat_width).astype(jnp.float32), mode="drop"
    )
    return placed.astype(jnp.bfloat16)


def solution(mesh):
    placed = (
        P("pts", "feat"),
        P(),
        P(("pts", "feat"), None),
        P("pts", None, None),
        P("pts", None),
        P("pts", None),
    )
    return jax.shard_map(
        local, mesh=mesh, in_specs=placed, out_specs=P("pts", "feat"), check_vma=False
    )
```

profile of v0, /device:TPU:0, one launch (start us, length us, event | category | flops | bytes accessed | tf_op | source)
XLA Modules:
  0.0 99.5 jit_solution(1397401444950790253)
XLA Ops:
  0.0 2.1 %copy.35 = bf16[24,4,8,512]{3,2,0,1:T(8,128)(2,1)} copy(bf16[24,4,8,512]{3,2,1,0:T(8,128)(2,1)} %bitcast.31) | data formatting | bytes 1572864 | tf_op jit(solution)/shard_map/reshape | solution.py:14
  2.1 4.2 %all-to-all-start = ((bf16[4,512,192]{1,2,0:T(8,128)(2,1)}), bf16[4,512,192]{1,2,0:T(8,128)(2,1)S(1)}, u32[]{:S(2)}, u32[]{:S(2)}) async-start(bf16[4,512,192]{1,2,0:T(8,128)(2,1)} %bitcast.29), calls=%async_computation | async-start | bytes 1572864 | tf_op jit(solution)/shard_map/all_to_all | solution.py:15
  6.3 1.4 %copy.28 = bf16[2048,192]{1,0:T(8,128)(2,1)S(1)} copy(bf16[2048,192]{0,1:T(8,128)(2,1)} %param.8) | data formatting | bytes 1572864 | tf_op args[0]
  7.8 0.7 compare_select_fusion.1
  8.4 0.8 copy.27
  9.2 0.7 compare_select_fusion
  9.9 0.1 copy.30
  10.0 0.1 reshape.185
  10.1 0.1 reshape_squeeze.6
  10.2 0.6 gather_fusion
  10.8 0.7 iota_compare_fusion
  11.5 0.7 iota_add_fusion
  12.3 0.1 add.119
  12.3 3.4 %scatter_custom_fusion.1 = f32[4096]{0:T(1024)S(1)} fusion(s32[512]{0:T(512)} %bitcast.35, f32[512]{0:T(512)S(1)} %broadcast.113, f32[]{:T(128)} %constant.22.clone.1), kind=kCustom, calls=%fused_computation.14 | custom fusion | flops 512 | bytes 16896 | tf_op jit(solution)/shard_map/scatter-add | solution.py:21
  15.8 4.1 %multiply_reduce_fusion = f32[4096]{0:T(1024)S(1)} fusion(bf16[4096,768]{1,0:T(8,128)(2,1)} %param.9), kind=kLoop, calls=%fused_computation.7 | loop fusion | flops 9433088 | bytes 6307840 | tf_op jit(solution)/shard_map/reduce_sum | solution.py:13
  19.9 0.2 multiply_reduce_fusion.1
  20.1 7.5 %subtract_reduce_fusion = f32[512]{0:T(512)S(1)} fusion(bf16[512,768]{0,1:T(8,128)(2,1)S(1)} %bitcast.32, bf16[4096,768]{1,0:T(8,128)(2,1)} %param.9, f32[4096]{0:T(1024)S(1)} %multiply_reduce_fusion, f32[512]{0:T(512)S(1)} %multiply_reduce_fusion.1), kind=kOutput, calls=%fused_computation.8 | convolution fusion | flops 3229613568 | bytes 7098368 | tf_op jit(solution)/shard_map/dot_general | solution.py:16
  27.6 3.3 %scatter_custom_fusion = f32[4096]{0:T(1024)S(1)} fusion(s32[512]{0:T(512)S(1)} %bitcast.36, f32[512]{0:T(512)S(1)} %subtract_reduce_fusion, f32[]{:T(128)} %constant.22.clone.1), kind=kCustom, calls=%fused_computation.16 | custom fusion | flops 512 | bytes 16388 | tf_op jit(solution)/shard_map/scatter-add | solution.py:20
  30.9 42.0 %all-reduce = (f32[4096]{0:T(1024)S(1)}, f32[4096]{0:T(1024)S(1)}) all-reduce(f32[4096]{0:T(1024)S(1)} %scatter_custom_fusion.1, f32[4096]{0:T(1024)S(1)} %scatter_custom_fusion), channel_id=1, replica_groups=mesh['pts'=8,'feat'=4] {'pts','feat'}, use_global_device_ids=true, to_apply=%region_6.8 | all-reduce | flops 8192 | bytes 65536 | tf_op jit(solution)/shard_map/psum | solution.py:22
  72.9 3.1 %gather_fusion.2 = f32[512]{0:T(512)S(1)} fusion(f32[4096]{0:T(1024)S(1)} %get-tuple-element.7, s32[1024]{0:T(1024)S(1)} %pad_clamp_fusion.1), kind=kCustom, calls=%fused_computation.clone | custom fusion | bytes 6144 | tf_op jit(solution)/shard_map/jit(_take)/gather | solution.py:23
  76.0 3.1 %gather_fusion.3 = f32[512]{0:T(512)S(1)} fusion(f32[4096]{0:T(1024)S(1)} %get-tuple-element.6, s32[1024]{0:T(1024)S(1)} %pad_clamp_fusion.1), kind=kCustom, calls=%fused_computation.1.clone | custom fusion | bytes 6144 | tf_op jit(solution)/shard_map/jit(_take)/gather | solution.py:23
  79.2 5.5 %all-gather = f32[4,1,512]{2,1,0:T(1,128)S(1)} all-gather(f32[1,1,512]{2,1,0:T(1,128)S(1)} %bitcast.33), channel_id=1, replica_groups=mesh['pts'=8,'feat'=4] {'feat'}, dimensions={0}, use_global_device_ids=true | all-gather | bytes 10240 | tf_op jit(solution)/shard_map/all_gather | solution.py:24
  84.7 0.7 gather_fusion.1
  85.4 0.1 reshape.184
  85.4 0.1 copy.31
  85.5 0.1 copy.32
  85.6 0.1 copy.26
  85.7 0.7 select_convert_fusion
  86.4 5.1 %all-to-all-start.1 = ((bf16[8,4,192]{2,1,0:T(4,128)(2,1)}), bf16[8,4,192]{2,1,0:T(4,128)(2,1)S(1)}, u32[]{:S(2)}, u32[]{:S(2)}) async-start(bf16[8,4,192]{2,1,0:T(4,128)(2,1)} %select_convert_fusion), calls=%async_computation.1 | async-start | bytes 32768 | tf_op jit(solution)/shard_map/all_to_all | solution.py:37
  91.5 6.6 %all-to-all-done.1 = bf16[8,4,192]{2,1,0:T(4,128)(2,1)S(1)} async-done(((bf16[8,4,192]{2,1,0:T(4,128)(2,1)}), bf16[8,4,192]{2,1,0:T(4,128)(2,1)S(1)}, u32[]{:S(2)}, u32[]{:S(2)}) %all-to-all-start.1) | async-done | bytes 12320 | tf_op jit(solution)/shard_map/all_to_all | solution.py:37
  98.1 0.8 scatter_custom_fusion.2
  98.9 0.6 convert_element_type.28
  (16 shorter events, 0.1 us)
Async XLA Ops:
  2.1 17.8 %all-to-all-start = ((bf16[4,512,192]{1,2,0:T(8,128)(2,1)}), bf16[4,512,192]{1,2,0:T(8,128)(2,1)S(1)}, u32[]{:S(2)}, u32[]{:S(2)}) async-start(bf16[4,512,192]{1,2,0:T(8,128)(2,1)} %bitcast.29), calls=%async_computation | async-start | bytes 1572864 | tf_op jit(solution)/shard_map/all_to_all | solution.py:15
  20.1 7.5 %copy-start.1 = (s32[512,1]{0,1:T(1,128)S(1)}, s32[512,1]{0,1:T(1,128)}, u32[]{:S(2)}) copy-start(s32[512,1]{0,1:T(1,128)} %param.10) | copy-start | bytes 6148
  27.6 57.9 %copy-start = (s32[1,8,4]{1,2,0:T(4,128)S(1)}, s32[1,8,4]{1,2,0:T(4,128)}, u32[]{:S(2)}) copy-start(s32[1,8,4]{1,2,0:T(4,128)} %param.11) | copy-start | bytes 388
  86.4 11.6 %all-to-all-start.1 = ((bf16[8,4,192]{2,1,0:T(4,128)(2,1)}), bf16[8,4,192]{2,1,0:T(4,128)(2,1)S(1)}, u32[]{:S(2)}, u32[]{:S(2)}) async-start(bf16[8,4,192]{2,1,0:T(4,128)(2,1)} %select_convert_fusion), calls=%async_computation.1 | async-start | bytes 32768 | tf_op jit(solution)/shard_map/all_to_all | solution.py:37
where the time goes:
time: 100 us; the launch traced here: 99.5 us
  blocking collectives  47.4 us (47%)
  other arithmetic  15.9 us (16%)
  local copies, waits for them, and re-layouts  12.6 us (13%)
  starting transfers between devices  9.3 us (9%)
  matrix products  7.52 us (8%)
  waiting for transfers between devices  6.57 us (7%)
    psum x1, blocking collectives, local(): lax.psum((cost_part, size_part), ('pts', 'feat'))  42 us
    dot_general x1, matrix products, local(): lax.dot_general(points, centres, contract, preferred_element_type=jnp.flo...  7.52 us
    all_to_all x1, waiting for transfers between devices, local(): lax.all_to_all(scaled, 'pts', split_axis=0, concat_axis=0, tiled=True)  6.57 us
    all_gather x1, blocking collectives, local(): shard_sens = lax.all_gather(own_sens, 'feat', axis=0, tiled=True)  5.45 us
    all_to_all x1, starting transfers between devices, local(): lax.all_to_all(scaled, 'pts', split_axis=0, concat_axis=0, tiled=True)  5.07 us
    all_to_all x1, starting transfers between devices, local(): lax.all_to_all(stacked, 'feat', split_axis=0, concat_axis=2, tiled=True)[0]  4.24 us
    reduce_sum x1, other arithmetic, local(): centre_sq = jnp.sum(jnp.square(centres.astype(jnp.float32)), axis=1)  4.09 us
    scatter-add x1, other arithmetic, local(): jax.ops.segment_sum(jnp.ones_like(nearest), member, num_segments=centre_c...  3.39 us
  transfers between devices with their start and end apart: 2, of which 1 were waited for; matrix products, arithmetic and copies ran while one was open for 14% of the time, Pallas kernels for 0%

commit v1 on v0

--- a/solution.py
+++ b/solution.py
@@ -1,7 +1,16 @@
+import functools
 import jax
 import jax.numpy as jnp
 from jax import lax
 from jax.sharding import PartitionSpec as P
+
+
+def direct_zone(panel, axis_name, peer_axis):
+    block_out = lax.psum(lax.psum(panel, axis_name), peer_axis)
+    return block_out
+
+
+measure_grid_now = functools.partial(direct_zone, axis_name="feat", peer_axis="pts")
 
 
 def local(slab, centres, labels, sample_rows, sample_count, slot_offset):
@@ -19,7 +28,7 @@
     member = labels[:, 0]
     cost_part = jax.ops.segment_sum(nearest, member, num_segments=centre_count)
     size_part = jax.ops.segment_sum(jnp.ones_like(nearest), member, num_segments=centre_count)
-    cluster_cost, cluster_size = lax.psum((cost_part, size_part), ("pts", "feat"))
+    cluster_cost, cluster_size = measure_grid_now((cost_part, size_part))
     own_sens = nearest / jnp.take(cluster_cost, member) + 1.0 / jnp.take(cluster_size, member)
     shard_sens = lax.all_gather(own_sens, "feat", axis=0, tiled=True)
     total_points = rows_pts * lax.axis_size("pts")

time: 100 us -> 106 us (1.060)
  blocking collectives: 47.4 us -> 55.2 us
  starting transfers between devices: 9.3 us -> 7.57 us
    psum x1 -> x2, blocking collectives: 42 us -> 50 us  [direct_zone(): block_out = lax.psum(lax.psum(panel, axis_name), peer_axis)]
    all_to_all x1, starting transfers between devices: 5.07 us -> 3.34 us  [local(): lax.all_to_all(scaled, 'pts', split_axis=0, concat_axis=0, tiled=True)]
  transfers between devices with their start and end apart: 2 -> 2, of which waited for: 1 -> 1; matrix products, arithmetic and copies ran while one was open for 14% -> 13% of each run, Pallas kernels for 0% -> 0%
where the time goes in v1:
time: 106 us; the launch traced here: 105 us
  blocking collectives  55.2 us (52%)
  other arithmetic  15.9 us (15%)
  local copies, waits for them, and re-layouts  12.6 us (12%)
  starting transfers between devices  7.57 us (7%)
  matrix products  7.52 us (7%)
  waiting for transfers between devices  6.5 us (6%)
    psum x2, blocking collectives, direct_zone(): block_out = lax.psum(lax.psum(panel, axis_name), peer_axis)  50 us
    dot_general x1, matrix products, local(): lax.dot_general(points, centres, contract, preferred_element_type=jnp.flo...  7.52 us
    all_to_all x1, waiting for transfers between devices, local(): lax.all_to_all(scaled, 'pts', split_axis=0, concat_axis=0, tiled=True)  6.5 us
    all_gather x1, blocking collectives, local(): shard_sens = lax.all_gather(own_sens, 'feat', axis=0, tiled=True)  5.19 us
    all_to_all x1, starting transfers between devices, local(): lax.all_to_all(stacked, 'feat', split_axis=0, concat_axis=2, tiled=True)[0]  4.24 us
    reduce_sum x1, other arithmetic, local(): centre_sq = jnp.sum(jnp.square(centres.astype(jnp.float32)), axis=1)  4.09 us
    scatter-add x1, other arithmetic, local(): jax.ops.segment_sum(jnp.ones_like(nearest), member, num_segments=centre_c...  3.39 us
    all_to_all x1, starting transfers between devices, local(): lax.all_to_all(scaled, 'pts', split_axis=0, concat_axis=0, tiled=True)  3.34 us
  transfers between devices with their start and end apart: 2, of which 1 were waited for; matrix products, arithmetic and copies ran while one was open for 13% of the time, Pallas kernels for 0%

profile of v1, /device:TPU:0, one launch (start us, length us, event | category | flops | bytes accessed | tf_op | source)
XLA Modules:
  0.0 105.5 jit_solution(10556144194741030771)
XLA Ops:
  0.0 2.1 %copy.35 = bf16[24,4,8,512]{3,2,0,1:T(8,128)(2,1)} copy(bf16[24,4,8,512]{3,2,1,0:T(8,128)(2,1)} %bitcast.31) | data formatting | bytes 1572864 | tf_op jit(solution)/shard_map/reshape | solution.py:23
  2.1 4.2 %all-to-all-start = ((bf16[4,512,192]{1,2,0:T(8,128)(2,1)}), bf16[4,512,192]{1,2,0:T(8,128)(2,1)S(1)}, u32[]{:S(2)}, u32[]{:S(2)}) async-start(bf16[4,512,192]{1,2,0:T(8,128)(2,1)} %bitcast.29), calls=%async_computation | async-start | bytes 1572864 | tf_op jit(solution)/shard_map/all_to_all | solution.py:24
  6.3 1.4 %copy.28 = bf16[2048,192]{1,0:T(8,128)(2,1)S(1)} copy(bf16[2048,192]{0,1:T(8,128)(2,1)} %param.8) | data formatting | bytes 1572864 | tf_op args[0]
  7.8 0.7 compare_select_fusion.1
  8.4 0.8 copy.27
  9.2 0.7 compare_select_fusion
  9.9 0.1 copy.30
  10.0 0.1 reshape.185
  10.2 0.6 gather_fusion
  10.8 0.7 iota_compare_fusion
  11.5 0.7 iota_add_fusion
  12.3 0.1 add.123
  12.3 3.4 %scatter_custom_fusion.1 = f32[4096]{0:T(1024)S(1)} fusion(s32[512]{0:T(512)} %bitcast.35, f32[512]{0:T(512)S(1)} %broadcast.113, f32[]{:T(128)} %constant.22.clone.1), kind=kCustom, calls=%fused_computation.14 | custom fusion | flops 512 | bytes 16896 | tf_op jit(solution)/shard_map/scatter-add | solution.py:30
  15.8 4.1 %multiply_reduce_fusion = f32[4096]{0:T(1024)S(1)} fusion(bf16[4096,768]{1,0:T(8,128)(2,1)} %param.9), kind=kLoop, calls=%fused_computation.7 | loop fusion | flops 9433088 | bytes 6307840 | tf_op jit(solution)/shard_map/reduce_sum | solution.py:22
  19.9 0.2 multiply_reduce_fusion.1
  20.1 7.5 %subtract_reduce_fusion = f32[512]{0:T(512)S(1)} fusion(bf16[512,768]{0,1:T(8,128)(2,1)S(1)} %bitcast.32, bf16[4096,768]{1,0:T(8,128)(2,1)} %param.9, f32[4096]{0:T(1024)S(1)} %multiply_reduce_fusion, f32[512]{0:T(512)S(1)} %multiply_reduce_fusion.1), kind=kOutput, calls=%fused_computation.8 | convolution fusion | flops 3229613568 | bytes 7098368 | tf_op jit(solution)/shard_map/dot_general | solution.py:25
  27.6 3.3 %scatter_custom_fusion = f32[4096]{0:T(1024)S(1)} fusion(s32[512]{0:T(512)S(1)} %bitcast.36, f32[512]{0:T(512)S(1)} %subtract_reduce_fusion, f32[]{:T(128)} %constant.22.clone.1), kind=kCustom, calls=%fused_computation.16 | custom fusion | flops 512 | bytes 16388 | tf_op jit(solution)/shard_map/scatter-add | solution.py:29
  30.9 12.1 %all-reduce.1 = (f32[4096]{0:T(1024)S(1)}, f32[4096]{0:T(1024)S(1)}) all-reduce(f32[4096]{0:T(1024)S(1)} %scatter_custom_fusion.1, f32[4096]{0:T(1024)S(1)} %scatter_custom_fusion), channel_id=1, replica_groups=mesh['pts'=8,'feat'=4] {'feat'}, use_global_device_ids=true, to_apply=%region_7.9 | all-reduce | flops 8192 | bytes 65536 | tf_op jit(solution)/shard_map/psum | solution.py:9
  43.0 37.9 %all-reduce = (f32[4096]{0:T(1024)S(1)}, f32[4096]{0:T(1024)S(1)}) all-reduce(f32[4096]{0:T(1024)S(1)} %get-tuple-element.8, f32[4096]{0:T(1024)S(1)} %get-tuple-element.9), channel_id=1, replica_groups=mesh['pts'=8,'feat'=4] {'pts'}, use_global_device_ids=true, to_apply=%region_8.10 | all-reduce | flops 8192 | bytes 65536 | tf_op jit(solution)/shard_map/psum | solution.py:9
  80.9 3.1 %gather_fusion.2 = f32[512]{0:T(512)S(1)} fusion(f32[4096]{0:T(1024)S(1)} %get-tuple-element.7, s32[1024]{0:T(1024)S(1)} %pad_clamp_fusion.1), kind=kCustom, calls=%fused_computation.clone | custom fusion | bytes 6144 | tf_op jit(solution)/shard_map/jit(_take)/gather | solution.py:32
  84.1 3.1 %gather_fusion.3 = f32[512]{0:T(512)S(1)} fusion(f32[4096]{0:T(1024)S(1)} %get-tuple-element.6, s32[1024]{0:T(1024)S(1)} %pad_clamp_fusion.1), kind=kCustom, calls=%fused_computation.1.clone | custom fusion | bytes 6144 | tf_op jit(solution)/shard_map/jit(_take)/gather | solution.py:32
  87.2 5.2 %all-gather = f32[4,1,512]{2,1,0:T(1,128)S(1)} all-gather(f32[1,1,512]{2,1,0:T(1,128)S(1)} %bitcast.33), channel_id=1, replica_groups=mesh['pts'=8,'feat'=4] {'feat'}, dimensions={0}, use_global_device_ids=true | all-gather | bytes 10240 | tf_op jit(solution)/shard_map/all_gather | solution.py:33
  92.4 0.7 gather_fusion.1
  93.1 0.1 reshape.184
  93.2 0.1 copy.31
  93.3 0.1 copy.32
  93.4 0.1 copy.26
  93.5 0.7 select_convert_fusion
  94.2 3.3 %all-to-all-start.1 = ((bf16[8,4,192]{2,1,0:T(4,128)(2,1)}), bf16[8,4,192]{2,1,0:T(4,128)(2,1)S(1)}, u32[]{:S(2)}, u32[]{:S(2)}) async-start(bf16[8,4,192]{2,1,0:T(4,128)(2,1)} %select_convert_fusion), calls=%async_computation.1 | async-start | bytes 32768 | tf_op jit(solution)/shard_map/all_to_all | solution.py:46
  97.6 6.5 %all-to-all-done.1 = bf16[8,4,192]{2,1,0:T(4,128)(2,1)S(1)} async-done(((bf16[8,4,192]{2,1,0:T(4,128)(2,1)}), bf16[8,4,192]{2,1,0:T(4,128)(2,1)S(1)}, u32[]{:S(2)}, u32[]{:S(2)}) %all-to-all-start.1) | async-done | bytes 12320 | tf_op jit(solution)/shard_map/all_to_all | solution.py:46
  104.1 0.8 scatter_custom_fusion.2
  104.9 0.6 convert_element_type.28
  (17 shorter events, 0.2 us)
Async XLA Ops:
  2.1 17.8 %all-to-all-start = ((bf16[4,512,192]{1,2,0:T(8,128)(2,1)}), bf16[4,512,192]{1,2,0:T(8,128)(2,1)S(1)}, u32[]{:S(2)}, u32[]{:S(2)}) async-start(bf16[4,512,192]{1,2,0:T(8,128)(2,1)} %bitcast.29), calls=%async_computation | async-start | bytes 1572864 | tf_op jit(solution)/shard_map/all_to_all | solution.py:24
  20.1 7.5 %copy-start.1 = (s32[512,1]{0,1:T(1,128)S(1)}, s32[512,1]{0,1:T(1,128)}, u32[]{:S(2)}) copy-start(s32[512,1]{0,1:T(1,128)} %param.10) | copy-start | bytes 6148
  27.6 65.7 %copy-start = (s32[1,8,4]{1,2,0:T(4,128)S(1)}, s32[1,8,4]{1,2,0:T(4,128)}, u32[]{:S(2)}) copy-start(s32[1,8,4]{1,2,0:T(4,128)} %param.11) | copy-start | bytes 388
  94.2 9.9 %all-to-all-start.1 = ((bf16[8,4,192]{2,1,0:T(4,128)(2,1)}), bf16[8,4,192]{2,1,0:T(4,128)(2,1)S(1)}, u32[]{:S(2)}, u32[]{:S(2)}) async-start(bf16[8,4,192]{2,1,0:T(4,128)(2,1)} %select_convert_fusion), calls=%async_computation.1 | async-start | bytes 32768 | tf_op jit(solution)/shard_map/all_to_all | solution.py:46
